TPU v7x, 512 devices: a whole 4x4x16 slice. The times are simulated.
512 devices in a mesh: dp: 16 (over x, y), tm: 32 (over z, core).
Axes of the slice: x: 4, y: 4, z: 16, core: 2. Of those that a mesh axis runs over, the one named last changes fastest.
Arguments:
- records: bfloat16 [16, 4096, 1024], P('dp', 'tm'), may hold values from -6 to 6
- x_weight: bfloat16 [1024, 512], replicated, may hold values from -0.1875 to 0.1875
- bc_weight: bfloat16 [1024, 256], replicated, may hold values from -0.1875 to 0.1875
- decay_codes: int32 [16, 4096, 8], P('dp', 'tm'), may hold values from 0 to 524
- out_grad: bfloat16 [16, 4096, 512], P('dp', 'tm'), may hold values from -6 to 6
Outputs:
- y_out: bfloat16 [16, 4096, 512], P('dp', 'tm')
- x_grad: float32 [1024, 512], P('tm')
- bc_grad: float32 [1024, 256], P('tm')
All inputs are finite; a program needn't handle non-finite values.
Results may differ from a plain program's by a relative error of at most 0.0085.
Values sent between devices are 32-bit elements; how exact they have to be, the bound alone decides.
No kernel may reach another device: no remote copies, remote signals or barrier semaphores. Data moves between devices by JAX's collectives and lax.ppermute only.
A program may use at most 64 MiB of HBM per device.

v0:
```python
import jax
import jax.numpy as jnp
from jax import lax
from jax.sharding import PartitionSpec as P

SPAN = 128
highest = lax.Precision.HIGHEST


def entering(part, axis, combine, identity, reverse):
    count = lax.axis_size(axis)
    place = lax.axis_index(axis)
    ahead = count - 1 - place if reverse else place
    gathered = jax.tree.map(lambda a: lax.all_gather(a, axis), part)
    state = jax.tree.map(lambda a, e: jnp.zeros_like(a) + jnp.asarray(e, a.dtype), part, identity)

    def one(turn, state):
        source = count - 1 - turn if reverse else turn
        return combine(
            state, jax.tree.map(lambda a: lax.dynamic_index_in_dim(a, source, 0, False), gathered)
        )

    return lax.fori_loop(0, ahead, one, state)


def span_kernel(log_decay):
    running = jnp.cumsum(log_decay, axis=1)
    length = log_decay.shape[1]
    causal = lax.broadcasted_iota(jnp.int32, (length, length), 0) >= lax.broadcasted_iota(
        jnp.int32, (length, length), 1
    )
    causal = causal[None, None, :, :]
    heads_first = jnp.transpose(running, (0, 2, 1))
    gaps = heads_first[:, :, :, None] - heads_first[:, :, None, :]
    kernel = jnp.where(causal, jnp.exp(jnp.where(causal, gaps, 0.0)), 0.0)
    return (running, kernel)


def block_scores(readout, inject):
    return jnp.einsum(
        "rtn,rsn->rts",
        readout.astype(jnp.bfloat16),
        inject.astype(jnp.bfloat16),
        preferred_element_type=jnp.float32,
    )


def forward_span(carry_state, pieces):
    mixer_f, inject, readout, cot_heads, log_decay = pieces
    running, kernel = span_kernel(log_decay)
    scores = block_scores(readout, inject)
    mixing = kernel * scores[:, None, :, :]
    decayed = jnp.exp(running)
    within = jnp.einsum("rhts,rshp->rthp", mixing, mixer_f, precision=highest)
    carried = decayed[..., None] * jnp.einsum(
        "rhpn,rtn->rthp", carry_state, readout, precision=highest
    )
    pair_dots = jnp.einsum("rthp,rshp->rhts", cot_heads, mixer_f, precision=highest)
    grad_read = jnp.einsum("rhts,rsn->rtn", kernel * pair_dots, inject, precision=highest)
    grad_read = grad_read + jnp.einsum(
        "rthp,rhpn->rtn", decayed[..., None] * cot_heads, carry_state, precision=highest
    )
    to_end = jnp.exp(running[:, -1:, :] - running)
    new_state = jnp.exp(running[:, -1, :])[:, :, None, None] * carry_state
    new_state = new_state + jnp.einsum(
        "rshp,rsn->rhpn", to_end[..., None] * mixer_f, inject, precision=highest
    )
    return (new_state, (within + carried, grad_read))


def reverse_span(adjoint, pieces):
    mixer_f, inject, readout, cot_heads, log_decay = pieces
    running, kernel = span_kernel(log_decay)
    scores = block_scores(readout, inject)
    mixing = kernel * scores[:, None, :, :]
    pair_dots = jnp.einsum("rthp,rshp->rhts", cot_heads, mixer_f, precision=highest)
    to_end = jnp.exp(running[:, -1:, :] - running)
    grad_mixer = jnp.einsum("rhts,rthp->rshp", mixing, cot_heads, precision=highest)
    grad_mixer = grad_mixer + to_end[..., None] * jnp.einsum(
        "rhpn,rsn->rshp", adjoint, inject, precision=highest
    )
    grad_inject = jnp.einsum("rhts,rtn->rsn", kernel * pair_dots, readout, precision=highest)
    grad_inject = grad_inject + jnp.einsum(
        "rshp,rhpn->rsn", to_end[..., None] * mixer_f, adjoint, precision=highest
    )
    new_adjoint = jnp.exp(running[:, -1, :])[:, :, None, None] * adjoint
    new_adjoint = new_adjoint + jnp.einsum(
        "rthp,rtn->rhpn", jnp.exp(running)[..., None] * cot_heads, readout, precision=highest
    )
    return (new_adjoint, (grad_mixer, grad_inject))


def to_blocks(array, frames):
    return array.reshape((frames // SPAN, 1, SPAN) + array.shape[1:])


def combine_pair(earlier, later_one):
    return (earlier[0] * later_one[0], later_one[0][:, :, None, None] * earlier[1] + later_one[1])


def body(records, x_weight, bc_weight, decay_codes, out_grad):
    signal = records[0]
    codes = decay_codes[0]
    frames_dev, model_dim = signal.shape
    head_count = codes.shape[1]
    mixer_dim = x_weight.shape[1]
    head_size = mixer_dim // head_count
    state_size = bc_weight.shape[1] // 2
    tm_count = lax.axis_size("tm")
    groups = lax.axis_size("dp")
    out_scale = (state_size * frames_dev * tm_count) ** (-0.5)
    grad_scale = (groups * frames_dev * tm_count) ** (-0.5)
    decay_unit = 1.0 / (32.0 * frames_dev * tm_count)
    mixer_in = jnp.dot(signal, x_weight, preferred_element_type=jnp.float32).astype(jnp.bfloat16)
    state_proj = jnp.dot(signal, bc_weight, preferred_element_type=jnp.float32).astype(jnp.bfloat16)
    log_decay = -decay_unit * codes.astype(jnp.float32)
    cotangent = out_grad[0].astype(jnp.float32) * out_scale
    mixer_f = mixer_in.astype(jnp.float32).reshape(frames_dev, head_count, head_size)
    inject = state_proj[:, :state_size].astype(jnp.float32)
    readout = state_proj[:, state_size:].astype(jnp.float32)
    cot_heads = cotangent.reshape(frames_dev, head_count, head_size)
    blocks = (
        to_blocks(mixer_f, frames_dev),
        to_blocks(inject, frames_dev),
        to_blocks(readout, frames_dev),
        to_blocks(cot_heads, frames_dev),
        to_blocks(log_decay, frames_dev),
    )
    zero_state = jnp.zeros((1, head_count, head_size, state_size), jnp.float32)
    end_state, (local_out, local_read) = lax.scan(forward_span, zero_state, blocks)
    start_adjoint, (local_grad, local_inject) = lax.scan(
        reverse_span, zero_state, blocks, reverse=True
    )
    running = jnp.cumsum(log_decay, axis=0)
    device_log = running[-1]
    identity = (jnp.ones((1, head_count), jnp.float32), zero_state)
    carry_in = entering(
        (jnp.exp(device_log)[None], end_state), "tm", combine_pair, identity, False
    )[1][0]
    adjoint_in = entering(
        (jnp.exp(device_log)[None], start_adjoint), "tm", combine_pair, identity, True
    )[1][0]
    decayed = jnp.exp(running)
    to_end = jnp.exp(device_log[None] - running)
    output = local_out.reshape(frames_dev, head_count, head_size)
    output = output + decayed[..., None] * jnp.einsum(
        "hpn,tn->thp", carry_in, readout, precision=highest
    )
    grad_read = local_read.reshape(frames_dev, state_size)
    grad_read = grad_read + jnp.einsum(
        "thp,hpn->tn", decayed[..., None] * cot_heads, carry_in, precision=highest
    )
    grad_mixer = local_grad.reshape(frames_dev, head_count, head_size)
    grad_mixer = grad_mixer + to_end[..., None] * jnp.einsum(
        "hpn,tn->thp", adjoint_in, inject, precision=highest
    )
    grad_inject = local_inject.reshape(frames_dev, state_size)
    grad_inject = grad_inject + jnp.einsum(
        "thp,hpn->tn", to_end[..., None] * mixer_f, adjoint_in, precision=highest
    )
    grad_mix = grad_mixer.reshape(frames_dev, mixer_dim).astype(jnp.bfloat16)
    grad_proj = jnp.concatenate([grad_inject, grad_read], axis=1).astype(jnp.bfloat16)
    grad_cat = jnp.concatenate([grad_mix, grad_proj], axis=1)
    grad_share = lax.psum_scatter(
        lax.dot_general(
            signal, grad_cat, (((0,), (0,)), ((), ())), preferred_element_type=jnp.float32
        ),
        "tm",
        scatter_dimension=0,
        tiled=True,
    )
    grad_share = lax.psum(grad_share, "dp")
    grad_share = grad_share * grad_scale
    y_out = output.reshape(frames_dev, mixer_dim).astype(jnp.bfloat16)[None]
    return (y_out, grad_share[:, :mixer_dim], grad_share[:, mixer_dim:])


def solution(mesh):
    return jax.shard_map(
        body,
        mesh=mesh,
        in_specs=(P("dp", "tm", None), P(), P(), P("dp", "tm", None), P("dp", "tm", None)),
        out_specs=(P("dp", "tm", None), P("tm", None), P("tm", None)),
        check_vma=False,
    )
```

profile of v0, /device:TPU:32, one launch (start us, length us, event | category | flops | bytes accessed | tf_op | source)
XLA Modules:
  0.0 444.9 jit_solution(17753559127679987640)
XLA Ops:
  9.1 1.4 convolution_convert_fusion.1
  10.5 1.3 convert_multiply_fusion
  15.5 33.9 %all-gather.3 = f32[32,1,8]{2,1,0:T(1,128)S(1)} all-gather(f32[1,1,8]{2,1,0:T(1,128)S(1)} %get-tuple-element.267), channel_id=2, replica_groups=mesh['dp'=16,'tm'=32] {'tm'}, dimensions={0}, use_global_device_ids=true | all-gather | bytes 1056 | tf_op jit(solution)/shard_map/all_gather | solution.py:14
  52.1 44.4 %all-gather.7.cloned.1.call-done = f32[256,64,128]{2,1,0:T(8,128)} async-done(((f32[8,64,128]{2,1,0:T(8,128)}), f32[256,64,128]{2,1,0:T(8,128)}) %all-gather.7.cloned.1.call-update) | async-done | bytes 8388624 | tf_op jit(solution)/shard_map/all_gather | solution.py:14
  96.6 2.2 while.16
  96.6 1.1 bitcast_add_fusion.4
  97.7 1.1 bitcast_add_fusion.4
  98.8 76.1 %all-gather.9.cloned.1.call-done = f32[256,64,128]{2,1,0:T(8,128)} async-done(((f32[8,64,128]{2,1,0:T(8,128)}), f32[256,64,128]{2,1,0:T(8,128)}) %all-gather.9.cloned.1.call-update) | async-done | bytes 8388624 | tf_op jit(solution)/shard_map/all_gather | solution.py:14
  174.9 31.9 %while.17 = (s32[]{:T(128)}, f32[1,8,64,128]{3,2,1,0:T(8,128)S(1)}, s32[]{:T(128)}, f32[32,1,8]{2,1,0:T(1,128)S(1)}, f32[32,1,8,64,128]{4,3,2,1,0:T(8,128)}, /*index=5*/s32[]{:T(128)}, s32[]{:T(128)}, s32[]{:T(128)}, s32[]{:T(128)}) while((s32[]{:T(128)}, f32[1,8,64,128]{3,2,1,0:T(8,128)S(1)}, s32[]{:T(128)}, f32[32,1,8]{2,1,0:T(1,128)S(1)}, ...), condition=%wide.region_5.6_spmd, body=%wide.region_4.5_spmd.sunk | while | flops 131078 | bytes 786683 | solution.py:23
  174.9 1.1 bitcast_add_fusion.5
  177.1 1.1 bitcast_add_fusion.5
  178.2 1.1 bitcast_add_fusion.5
  180.4 1.1 bitcast_add_fusion.5
  182.6 1.1 bitcast_add_fusion.5
  183.7 1.1 bitcast_add_fusion.5
  185.9 1.1 bitcast_add_fusion.5
  187.0 1.1 bitcast_add_fusion.5
  189.2 1.1 bitcast_add_fusion.5
  191.5 1.1 bitcast_add_fusion.5
  192.6 1.1 bitcast_add_fusion.5
  194.8 1.1 bitcast_add_fusion.5
  195.9 1.1 bitcast_add_fusion.5
  198.1 1.1 bitcast_add_fusion.5
  199.2 1.1 bitcast_add_fusion.5
  201.4 1.1 bitcast_add_fusion.5
  203.6 1.1 bitcast_add_fusion.5
  204.7 1.1 bitcast_add_fusion.5
  208.8 2.2 convolution_bitcast_fusion
  211.1 3.5 copy.87
  215.7 101.2 %reduce-scatter.4.cloned.1.call-done = f32[32,768]{1,0:T(8,128)} async-done(((f32[1024,768]{1,0:T(8,128)}), f32[32,768]{1,0:T(8,128)}) %reduce-scatter.4.cloned.1.call-update) | async-done | bytes 98320
  316.9 1.8 copy.88
  319.7 116.2 %all-reduce.2.cloned.1.call-done = f32[32,768]{0,1:T(8,128)} async-done(((f32[32,768]{0,1:T(8,128)}), f32[32,768]{0,1:T(8,128)}) %all-reduce.2.cloned.1.call-update) | async-done | bytes 98320 | tf_op jit(solution)/shard_map/psum | solution.py:172
  (102 shorter events, 26.7 us)
Async XLA Ops:
  7.2 3.3 copy-start
  7.2 89.4 %all-gather.7.cloned.1.call-start = ((), (), s32[]{:S(2)}) async-start(), calls=%async_computation.2 | async-start | bytes 8650752 | tf_op jit(solution)/shard_map/all_gather | solution.py:14
  12.9 161.9 %all-gather.9.cloned.1.call-start = ((), (), s32[]{:S(2)}) async-start(), calls=%async_computation.3 | async-start | bytes 8650752 | tf_op jit(solution)/shard_map/all_gather | solution.py:14
  14.1 194.7 %copy-start.1 = (bf16[1,128,1024]{2,1,0:T(8,128)(2,1)S(1)}, bf16[1,128,1024]{2,1,0:T(8,128)(2,1)}, u32[]{:S(2)}) copy-start(bf16[1,128,1024]{2,1,0:T(8,128)(2,1)} %param.9) | copy-start | bytes 786436
  15.1 301.7 %reduce-scatter.4.cloned.1.call-start = ((), (), s32[]{:S(2)}) async-start(), calls=%async_computation.4 | async-start | bytes 3244032
  214.6 221.3 %all-reduce.2.cloned.1.call-start = ((), (), s32[]{:S(2)}) async-start(), calls=%async_computation.1 | async-start | bytes 786432 | tf_op jit(solution)/shard_map/psum | solution.py:172
Sparse Core Ops, SparseCore 0:
  13.0 83.4 all-gather.6
  98.7 76.1 all-gather.8
  214.7 102.0 reduce-scatter.3
  320.3 115.5 all-reduce.1
where the time goes:
time: 446 us; the launch traced here: 445 us
  waiting for transfers between devices  338 us (76%)
  other arithmetic  35.2 us (8%)
  blocking collectives  33.9 us (8%)
  between operations  14 us (3%)
  matrix products  12.6 us (3%)
  local copies, waits for them, and re-layouts  10 us (2%)
    all_gather x2, waiting for transfers between devices, entering(): gathered = jax.tree.map(lambda a: lax.all_gather(a, axis), part)  121 us
    psum x1, waiting for transfers between devices, body(): grad_share = lax.psum(grad_share, 'dp')  116 us
    unnamed x5, waiting for transfers between devices  101 us
    all_gather x1, blocking collectives, entering(): gathered = jax.tree.map(lambda a: lax.all_gather(a, axis), part)  33.9 us
    add x31, other arithmetic, combine_pair(): later_one[0][:, :, None, None] * earlier[1] + later_one[1]  32.9 us
  transfers between devices with their start and end apart: 4, of which 4 were waited for; matrix products, arithmetic and copies ran while one was open for 2% of the time, Pallas kernels for 0%

commit v1 on v0

--- a/solution.py
+++ b/solution.py
@@ -5,6 +5,14 @@
 
 SPAN = 128
 highest = lax.Precision.HIGHEST
+
+
+def doubling_sum(shard, axis):
+    n_dev, total = (lax.axis_size(axis), shard)
+    for reach in [1 << k for k in range(n_dev.bit_length() - 1)]:
+        pairs = [(i, i ^ reach) for i in range(n_dev)]
+        total = total + lax.ppermute(total, axis, pairs)
+    return total
 
 
 def entering(part, axis, combine, identity, reverse):
@@ -169,7 +177,7 @@
         scatter_dimension=0,
         tiled=True,
     )
-    grad_share = lax.psum(grad_share, "dp")
+    grad_share = doubling_sum(grad_share, "dp")
     grad_share = grad_share * grad_scale
     y_out = output.reshape(frames_dev, mixer_dim).astype(jnp.bfloat16)[None]
     return (y_out, grad_share[:, :mixer_dim], grad_share[:, mixer_dim:])

time: 446 us -> 379 us (0.85)
  the two profiles are of different devices: /device:TPU:32 before, /device:TPU:96 now
where the time goes in v1:
time: 379 us; the launch traced here: 378 us
  waiting for transfers between devices  261 us (69%)
  other arithmetic  34.4 us (9%)
  blocking collectives  30.9 us (8%)
  starting transfers between devices  14.6 us (4%)
  between operations  14.1 us (4%)
  matrix products  12.7 us (3%)
  local copies, waits for them, and re-layouts  9.25 us (2%)
    all_gather x2, waiting for transfers between devices, entering(): gathered = jax.tree.map(lambda a: lax.all_gather(a, axis), part)  117 us
    unnamed x4, waiting for transfers between devices  107 us
    ppermute x4, waiting for transfers between devices, doubling_sum(): total = total + lax.ppermute(total, axis, pairs)  37 us
    add x31, other arithmetic, combine_pair(): later_one[0][:, :, None, None] * earlier[1] + later_one[1]  32.9 us
    all_gather x1, blocking collectives, entering(): gathered = jax.tree.map(lambda a: lax.all_gather(a, axis), part)  30.9 us
    ppermute x4, starting transfers between devices, doubling_sum(): total = total + lax.ppermute(total, axis, pairs)  14.4 us
    unnamed x10, local copies, waits for them, and re-layouts  7.82 us
  transfers between devices with their start and end apart: 7, of which 7 were waited for; matrix products, arithmetic and copies ran while one was open for 4% of the time, Pallas kernels for 0%

profile of v1, /device:TPU:96, one launch (start us, length us, event | category | flops | bytes accessed | tf_op | source)
XLA Modules:
  0.0 377.7 jit_solution(9484812434733328361)
XLA Ops:
  9.1 1.4 convolution_convert_fusion.1
  10.5 1.3 convert_multiply_fusion
  15.5 30.9 %all-gather.3 = f32[32,1,8]{2,1,0:T(1,128)S(1)} all-gather(f32[1,1,8]{2,1,0:T(1,128)S(1)} %get-tuple-element.267), channel_id=2, replica_groups=mesh['dp'=16,'tm'=32] {'tm'}, dimensions={0}, use_global_device_ids=true | all-gather | bytes 1056 | tf_op jit(solution)/shard_map/all_gather | solution.py:22
  49.1 45.6 %all-gather.7.cloned.1.call-done = f32[256,64,128]{2,1,0:T(8,128)} async-done(((f32[8,64,128]{2,1,0:T(8,128)}), f32[256,64,128]{2,1,0:T(8,128)}) %all-gather.7.cloned.1.call-update) | async-done | bytes 8388624 | tf_op jit(solution)/shard_map/all_gather | solution.py:22
  94.8 6.6 %while.16 = (s32[]{:T(128)}, f32[1,8,64,128]{3,2,1,0:T(8,128)S(1)}, s32[]{:T(128)}, f32[32,1,8]{2,1,0:T(1,128)S(1)}, f32[32,1,8,64,128]{4,3,2,1,0:T(8,128)}, /*index=5*/s32[]{:T(128)}, s32[]{:T(128)}, s32[]{:T(128)}) while((s32[]{:T(128)}, f32[1,8,64,128]{3,2,1,0:T(8,128)S(1)}, s32[]{:T(128)}, f32[32,1,8]{2,1,0:T(1,128)S(1)}, ...), condition=%wide.region_3.4_spmd, body=%wide.region_2.3_spmd.sunk | while | flops 131077 | bytes 786663 | solution.py:31
  94.8 1.1 bitcast_add_fusion.4
  97.0 1.1 bitcast_add_fusion.4
  99.2 1.1 bitcast_add_fusion.4
  100.3 1.1 bitcast_add_fusion.4
  101.4 71.6 %all-gather.9.cloned.1.call-done = f32[256,64,128]{2,1,0:T(8,128)} async-done(((f32[8,64,128]{2,1,0:T(8,128)}), f32[256,64,128]{2,1,0:T(8,128)}) %all-gather.9.cloned.1.call-update) | async-done | bytes 8388624 | tf_op jit(solution)/shard_map/all_gather | solution.py:22
  173.0 27.5 %while.17 = (s32[]{:T(128)}, f32[1,8,64,128]{3,2,1,0:T(8,128)S(1)}, s32[]{:T(128)}, f32[32,1,8]{2,1,0:T(1,128)S(1)}, f32[32,1,8,64,128]{4,3,2,1,0:T(8,128)}, /*index=5*/s32[]{:T(128)}, s32[]{:T(128)}, s32[]{:T(128)}, s32[]{:T(128)}) while((s32[]{:T(128)}, f32[1,8,64,128]{3,2,1,0:T(8,128)S(1)}, s32[]{:T(128)}, f32[32,1,8]{2,1,0:T(1,128)S(1)}, ...), condition=%wide.region_5.6_spmd, body=%wide.region_4.5_spmd.sunk | while | flops 131078 | bytes 786683 | solution.py:31
  173.1 1.1 bitcast_add_fusion.5
  175.3 1.1 bitcast_add_fusion.5
  177.5 1.1 bitcast_add_fusion.5
  178.6 1.1 bitcast_add_fusion.5
  180.8 1.1 bitcast_add_fusion.5
  181.9 1.1 bitcast_add_fusion.5
  184.1 1.1 bitcast_add_fusion.5
  185.2 1.1 bitcast_add_fusion.5
  187.4 1.1 bitcast_add_fusion.5
  189.6 1.1 bitcast_add_fusion.5
  202.6 2.2 convolution_bitcast_fusion
  204.8 3.5 copy.87
  208.3 106.5 %reduce-scatter.4.cloned.1.call-done = f32[32,768]{1,0:T(8,128)} async-done(((f32[1024,768]{1,0:T(8,128)}), f32[32,768]{1,0:T(8,128)}) %reduce-scatter.4.cloned.1.call-update) | async-done | bytes 98320
  315.9 3.0 collective-permute-start
  318.9 8.4 %collective-permute-done = f32[32,768]{0,1:T(8,128)S(1)} collective-permute-done((f32[32,768]{0,1:T(8,128)S(1)}, f32[32,768]{0,1:T(8,128)S(1)}, u32[]{:S(2)}, u32[]{:S(2)}) %collective-permute-start) | collective-permute-done | bytes 98336 | tf_op jit(solution)/shard_map/ppermute | solution.py:14
  327.4 4.5 %collective-permute-start.1 = (f32[32,768]{0,1:T(8,128)S(1)}, f32[32,768]{0,1:T(8,128)S(1)}, u32[]{:S(2)}, u32[]{:S(2)}) collective-permute-start(f32[32,768]{0,1:T(8,128)S(1)} %add.107), channel_id=1, source_target_pairs={{0,64},{32,96},{64,0},{96,32},{128,192},{160,224},{192,128},{224,1... | collective-permute-start | bytes 294920 | tf_op jit(solution)/shard_map/ppermute | solution.py:14
  332.1 9.2 %collective-permute-done.1 = f32[32,768]{0,1:T(8,128)S(1)} collective-permute-done((f32[32,768]{0,1:T(8,128)S(1)}, f32[32,768]{0,1:T(8,128)S(1)}, u32[]{:S(2)}, u32[]{:S(2)}) %collective-permute-start.1) | collective-permute-done | bytes 98336 | tf_op jit(solution)/shard_map/ppermute | solution.py:14
  341.4 2.5 collective-permute-start.2
  344.7 10.4 %collective-permute-done.2 = f32[32,768]{0,1:T(8,128)S(1)} collective-permute-done((f32[32,768]{0,1:T(8,128)S(1)}, f32[32,768]{0,1:T(8,128)S(1)}, u32[]{:S(2)}, u32[]{:S(2)}) %collective-permute-start.2) | collective-permute-done | bytes 98336 | tf_op jit(solution)/shard_map/ppermute | solution.py:14
  355.1 4.5 %collective-permute-start.3 = (f32[32,768]{0,1:T(8,128)S(1)}, f32[32,768]{0,1:T(8,128)S(1)}, u32[]{:S(2)}, u32[]{:S(2)}) collective-permute-start(f32[32,768]{0,1:T(8,128)S(1)} %add.109), channel_id=1, source_target_pairs={{0,256},{32,288},{64,320},{96,352},{128,384},{160,416},{192,448},{... | collective-permute-start | bytes 294920 | tf_op jit(solution)/shard_map/ppermute | solution.py:14
  360.7 9.0 %collective-permute-done.3 = f32[32,768]{0,1:T(8,128)S(1)} collective-permute-done((f32[32,768]{0,1:T(8,128)S(1)}, f32[32,768]{0,1:T(8,128)S(1)}, u32[]{:S(2)}, u32[]{:S(2)}) %collective-permute-start.3) | collective-permute-done | bytes 98336 | tf_op jit(solution)/shard_map/ppermute | solution.py:14
  (110 shorter events, 33.2 us)
Async XLA Ops:
  7.2 3.3 copy-start
  7.2 87.6 %all-gather.7.cloned.1.call-start = ((), (), s32[]{:S(2)}) async-start(), calls=%async_computation.1 | async-start | bytes 8650752 | tf_op jit(solution)/shard_map/all_gather | solution.py:22
  12.9 160.1 %all-gather.9.cloned.1.call-start = ((), (), s32[]{:S(2)}) async-start(), calls=%async_computation.2 | async-start | bytes 8650752 | tf_op jit(solution)/shard_map/all_gather | solution.py:22
  14.1 188.5 %copy-start.1 = (bf16[1,128,1024]{2,1,0:T(8,128)(2,1)S(1)}, bf16[1,128,1024]{2,1,0:T(8,128)(2,1)}, u32[]{:S(2)}) copy-start(bf16[1,128,1024]{2,1,0:T(8,128)(2,1)} %param.9) | copy-start | bytes 786436
  15.1 299.7 %reduce-scatter.4.cloned.1.call-start = ((), (), s32[]{:S(2)}) async-start(), calls=%async_computation.3 | async-start | bytes 3244032
  315.9 11.4 %collective-permute-start = (f32[32,768]{0,1:T(8,128)S(1)}, f32[32,768]{0,1:T(8,128)S(1)}, u32[]{:S(2)}, u32[]{:S(2)}) collective-permute-start(f32[32,768]{0,1:T(8,128)S(1)} %copy.88), channel_id=1, source_target_pairs={{0,32},{32,0},{64,96},{96,64},{128,160},{160,128},{192,224},{224,1... | collective-permute-start | bytes 294920 | tf_op jit(solution)/shard_map/ppermute | solution.py:14
  327.4 14.0 %collective-permute-start.1 = (f32[32,768]{0,1:T(8,128)S(1)}, f32[32,768]{0,1:T(8,128)S(1)}, u32[]{:S(2)}, u32[]{:S(2)}) collective-permute-start(f32[32,768]{0,1:T(8,128)S(1)} %add.107), channel_id=1, source_target_pairs={{0,64},{32,96},{64,0},{96,32},{128,192},{160,224},{192,128},{224,1... | collective-permute-start | bytes 294920 | tf_op jit(solution)/shard_map/ppermute | solution.py:14
  341.4 13.6 %collective-permute-start.2 = (f32[32,768]{0,1:T(8,128)S(1)}, f32[32,768]{0,1:T(8,128)S(1)}, u32[]{:S(2)}, u32[]{:S(2)}) collective-permute-start(f32[32,768]{0,1:T(8,128)S(1)} %add.108), channel_id=1, source_target_pairs={{0,128},{32,160},{64,192},{96,224},{128,0},{160,32},{192,64},{224,... | collective-permute-start | bytes 294920 | tf_op jit(solution)/shard_map/ppermute | solution.py:14
  355.1 14.5 %collective-permute-start.3 = (f32[32,768]{0,1:T(8,128)S(1)}, f32[32,768]{0,1:T(8,128)S(1)}, u32[]{:S(2)}, u32[]{:S(2)}) collective-permute-start(f32[32,768]{0,1:T(8,128)S(1)} %add.109), channel_id=1, source_target_pairs={{0,256},{32,288},{64,320},{96,352},{128,384},{160,416},{192,448},{... | collective-permute-start | bytes 294920 | tf_op jit(solution)/shard_map/ppermute | solution.py:14
Sparse Core Ops, SparseCore 0:
  13.0 81.6 all-gather.6
  96.9 76.1 all-gather.8
  208.5 106.3 reduce-scatter.3
